TPU v7x, 32 devices: a whole 2x2x4 slice. The times are simulated.
32 devices in a mesh: grp: 2 (over y), row: 8 (over z, core), col: 2 (over x).
Axes of the slice: x: 2, y: 2, z: 4, core: 2. Of those that a mesh axis runs over, the one named last changes fastest.
Arguments:
- pair: bfloat16 [192, 96, 128], P(('grp', 'row'), 'col'), parts along dimension 0, may hold values from -6 to 6
- token_count: int32 [2], P('grp'), parts along dimension 0, may hold values from 72 to 96
- tri_in: bfloat16 [2, 128, 512], replicated, may hold values from -0.5 to 0.5
- tri_gate: bfloat16 [2, 128, 128], replicated, may hold values from -0.5 to 0.5
- tri_out: bfloat16 [2, 128, 128], replicated, may hold values from -0.5 to 0.5
- trans_in: bfloat16 [128, 1024], replicated, may hold values from -0.5 to 0.5
- trans_out: bfloat16 [512, 128], replicated, may hold values from -0.25 to 0.25
Outputs:
- pair_out: bfloat16 [192, 96, 128], P(('grp', 'row'), 'col'), parts along dimension 0
There are 2 independent parts, one for each index of `grp`. A program takes and returns all parts, laid end to end along the dimension named above; an argument that names none is the same for every part. Nothing has to cross between parts.
Inputs may be any that keep to these rules, and one draw needn't show every extreme that they name: `token_count`: the number of real tokens of the complex; pair entries with either token index at or past it are padding.
All inputs are finite; a program needn't handle non-finite values.
Results may differ from a plain program's by a relative error of at most 0.015.
Values may be sent and summed in bfloat16 or wider, within the bound.
No kernel may reach another device: no remote copies, remote signals or barrier semaphores. Data moves between devices by JAX's collectives and lax.ppermute only.
A program may use at most 64 MiB of HBM per device.

v0:
```python
import jax
import jax.numpy as jnp
from jax import lax
from jax.sharding import PartitionSpec as P


def layer_norm(values, along):
    average = jnp.mean(values, axis=along, keepdims=True)
    centred = values - average
    spread = jnp.mean(centred * centred, axis=along, keepdims=True)
    return centred * lax.rsqrt(spread + 1e-05)


def contract_rows(left_side, right_side):
    return jnp.einsum("hik,hjk->hij", left_side, right_side, preferred_element_type=jnp.float32)


def contract_columns(left_side, right_side):
    return jnp.einsum("hki,hkj->hij", left_side, right_side, preferred_element_type=jnp.float32)


def body(pair, token_count, tri_in, tri_gate, tri_out, trans_in, trans_out):
    tile_rows, tile_cols, pair_width = pair.shape
    hidden = tri_out.shape[1]
    ffn_width = trans_out.shape[0]
    row_place = lax.axis_index("row")
    col_place = lax.axis_index("col")
    row_first = row_place * tile_rows
    col_first = col_place * tile_cols
    token_limit = token_count[0]
    row_keep = (row_first + jnp.arange(tile_rows, dtype=jnp.int32) < token_limit).astype(
        jnp.float32
    )
    col_keep = (col_first + jnp.arange(tile_cols, dtype=jnp.int32) < token_limit).astype(
        jnp.float32
    )
    keep_mask = row_keep[:, None] * col_keep[None, :]

    def project(stream, which_side):
        normed = layer_norm(stream.astype(jnp.float32), 2).astype(jnp.bfloat16)
        weight = tri_in[which_side].reshape(pair_width, 4, hidden)
        projected = jnp.einsum("ijc,cgh->ghij", normed, weight, preferred_element_type=jnp.float32)
        left_side = (keep_mask * jax.nn.sigmoid(projected[2]) * projected[0]).astype(jnp.bfloat16)
        right_side = (keep_mask * jax.nn.sigmoid(projected[3]) * projected[1]).astype(jnp.bfloat16)
        gate_value = jax.nn.sigmoid(
            jnp.dot(normed, tri_gate[which_side], preferred_element_type=jnp.float32)
        )
        return (left_side, right_side, gate_value)

    def finish(stream, mixed_sum, gate_value, which_side):
        normed = layer_norm(mixed_sum, 0).astype(jnp.bfloat16)
        update = gate_value * jnp.einsum(
            "hij,hc->ijc", normed, tri_out[which_side], preferred_element_type=jnp.float32
        )
        return (stream.astype(jnp.float32) + keep_mask[:, :, None] * update).astype(jnp.bfloat16)

    left_side, right_side, gate_value = project(pair, 0)
    partial_rows = contract_rows(left_side, lax.all_gather(right_side, "row", axis=1, tiled=True))
    mixed_sum = lax.psum_scatter(partial_rows, "col", scatter_dimension=2, tiled=True)
    stream = finish(pair, mixed_sum, gate_value, 0)
    left_side, right_side, gate_value = project(stream, 1)
    left_rows = lax.all_gather(left_side, "col", axis=2, tiled=True)
    column_strip = lax.all_to_all(left_rows, "row", split_axis=2, concat_axis=1, tiled=True)
    mixed_sum = contract_columns(
        column_strip, lax.all_gather(right_side, "row", axis=1, tiled=True)
    )
    stream = finish(stream, mixed_sum, gate_value, 1)
    normed = layer_norm(stream.astype(jnp.float32), 2).astype(jnp.bfloat16)
    inner_sum = jnp.dot(normed, trans_in, preferred_element_type=jnp.float32)
    activation = (jax.nn.silu(inner_sum[..., :ffn_width]) * inner_sum[..., ffn_width:]).astype(
        jnp.bfloat16
    )
    update = jnp.dot(activation, trans_out, preferred_element_type=jnp.float32)
    return (stream.astype(jnp.float32) + keep_mask[:, :, None] * update).astype(jnp.bfloat16)


def solution(mesh):
    placed = (P(("grp", "row"), "col", None), P("grp"), P(), P(), P(), P(), P())
    return jax.shard_map(
        body, mesh=mesh, in_specs=placed, out_specs=P(("grp", "row"), "col", None), check_vma=False
    )
```

profile of v0, /device:TPU:0, one launch (start us, length us, event | category | flops | bytes accessed | tf_op | source)
XLA Modules:
  0.0 121.3 jit_solution(946812768014044533)
XLA Ops:
  7.2 1.1 convert_reduce_fusion
  8.3 1.2 fusion.21
  9.5 1.6 %fusion.72 = (bf16[1,128,512]{2,1,0:T(8,128)(2,1)}, bf16[1,128,512]{2,1,0:T(8,128)(2,1)S(1)}) fusion(bf16[2,128,512]{2,1,0:T(8,128)(2,1)} %param.9), kind=kLoop, calls=%fused_computation.108 | loop fusion | bytes 524288 | tf_op jit(solution)/shard_map/slice | solution.py:41
  11.2 0.1 copy.110
  11.3 0.1 broadcast_multiply_fusion.5
  11.4 0.4 convolution_bitcast_fusion.1
  11.8 0.9 fusion.38
  12.7 0.0 all-gather.3.cloned.1.call-update
  12.7 0.0 reduce-scatter.2.cloned.1.call-start
  12.7 1.2 %copy.84 = bf16[128,12,48]{2,1,0:T(8,128)(2,1)} copy(bf16[128,12,48]{0,2,1:T(8,128)(2,1)S(1)} %get-tuple-element.8) | data formatting | bytes 294912 | tf_op jit(solution)/shard_map/convert_element_type | solution.py:43
  14.0 24.4 %all-gather.3.cloned.1.call-done = bf16[128,96,48]{0,2,1:T(8,128)(2,1)} async-done(((bf16[128,12,48]{0,2,1:T(8,128)(2,1)}), bf16[128,96,48]{0,2,1:T(8,128)(2,1)}) %all-gather.3.cloned.1.call-update) | async-done | bytes 1179664 | tf_op jit(solution)/shard_map/all_gather | solution.py:58
  38.3 5.3 %copy.85 = bf16[128,96,48]{2,1,0:T(8,128)(2,1)S(1)} copy(bf16[128,96,48]{0,2,1:T(8,128)(2,1)} %all-gather.3.cloned.1.call-done) | data formatting | bytes 2359296 | tf_op jit(solution)/shard_map/all_gather | solution.py:58
  43.6 3.7 %fusion.76 = f32[128,12,96]{2,1,0:T(8,128)} fusion(bf16[128,12,48]{2,1,0:T(8,128)(2,1)} %copy.84, bf16[128,96,48]{2,1,0:T(8,128)(2,1)S(1)} %copy.85), kind=kOutput, calls=%fused_computation.112 | convolution fusion | flops 14155776 | bytes 1916928 | tf_op jit(solution)/shard_map/hik,hjk->hij/dot_general | solution.py:15
  47.4 2.7 %copy.86 = f32[128,12,96]{0,1,2:T(8,128)} copy(f32[128,12,96]{2,1,0:T(8,128)} %fusion.76) | data formatting | bytes 1179648 | tf_op jit(solution)/shard_map/hik,hjk->hij/dot_general | solution.py:15
  50.1 0.0 reduce-scatter.2.cloned.1.call-update
  50.2 0.0 all-gather.5.cloned.1.call-start
  50.2 0.1 copy.114
  50.4 0.3 fusion.11
  50.7 16.7 %reduce-scatter.2.cloned.1.call-done = f32[128,12,48]{0,1,2:T(8,128)} async-done(((f32[128,12,96]{0,1,2:T(8,128)}), f32[128,12,48]{0,1,2:T(8,128)}) %reduce-scatter.2.cloned.1.call-update) | async-done | bytes 294928 | tf_op jit(solution)/shard_map/reduce_scatter | solution.py:59
  67.5 1.2 %reduce_sum.92 = f32[12,48]{0,1:T(8,128)S(1)} reduce(f32[128,12,48]{0,1,2:T(8,128)} %reduce-scatter.2.cloned.1.call-done, f32[]{:T(128)} %constant.32.clone.1), dimensions={0}, to_apply=%region_3.0 | reduce | flops 73152 | bytes 297220 | tf_op jit(solution)/shard_map/reduce_sum | solution.py:8
  68.7 0.1 copy.87
  68.8 0.1 copy.88
  68.9 1.3 %multiply_reduce_fusion.1 = f32[12,48]{0,1:T(8,128)S(1)} fusion(f32[128,12,48]{0,1,2:T(8,128)} %reduce-scatter.2.cloned.1.call-done, f32[12,48]{0,1:T(8,128)S(1)} %copy.88), kind=kLoop, calls=%fused_computation.31 | loop fusion | flops 220608 | bytes 299520 | tf_op jit(solution)/shard_map/reduce_sum | solution.py:10
  70.2 0.1 copy.89
  70.3 0.1 copy.90
  70.4 0.3 multiply_convert_fusion.1
  70.7 0.3 fusion.73
  71.0 0.3 multiply_reduce_fusion.3
  71.3 0.4 convolution_bitcast_fusion
  71.7 0.9 fusion.24
  72.6 6.1 %all_gather.10 = bf16[128,12,96]{0,2,1:T(8,128)(2,1)S(1)} all-gather(bf16[128,12,48]{0,2,1:T(8,128)(2,1)S(1)} %get-tuple-element.6), channel_id=1, replica_groups=mesh['grp'=2,'row'=8,'col'=2] {'col'}, dimensions={2}, use_global_device_ids=true | all-gather | bytes 442368 | tf_op jit(solution)/shard_map/all_gather | solution.py:62
  78.6 0.9 copy.95
  79.5 4.6 %all-to-all-start = ((bf16[128,12,96]{0,1,2:T(8,128)(2,1)}), bf16[128,12,96]{0,1,2:T(8,128)(2,1)S(1)}, u32[]{:S(2)}, u32[]{:S(2)}) async-start(bf16[128,12,96]{0,1,2:T(8,128)(2,1)} %copy.95), calls=%async_computation.1 | async-start | bytes 786432 | tf_op jit(solution)/shard_map/all_to_all | solution.py:63
  84.1 1.1 fusion.8
  85.2 17.1 %all-to-all-done = bf16[128,12,96]{0,1,2:T(8,128)(2,1)S(1)} async-done(((bf16[128,12,96]{0,1,2:T(8,128)(2,1)}), bf16[128,12,96]{0,1,2:T(8,128)(2,1)S(1)}, u32[]{:S(2)}, u32[]{:S(2)}) %all-to-all-start) | async-done | bytes 294944 | tf_op jit(solution)/shard_map/all_to_all | solution.py:63
  102.3 0.1 all_to_all.16
  102.4 1.2 %copy.98 = bf16[128,96,12]{1,2,0:T(8,128)(2,1)} copy(bf16[128,96,12]{0,1,2:T(8,128)(2,1)S(1)} %all_to_all.16) | data formatting | bytes 589824 | tf_op jit(solution)/shard_map/all_to_all | solution.py:63
  103.7 5.3 %copy.99 = bf16[128,96,48]{2,1,0:T(8,128)(2,1)S(1)} copy(bf16[128,96,48]{0,2,1:T(8,128)(2,1)} %all-gather.5.cloned.1.call-done) | data formatting | bytes 2359296 | tf_op jit(solution)/shard_map/all_gather | solution.py:65
  109.0 2.0 %fusion.74 = (f32[12,48]{1,0:T(8,128)S(1)}, f32[128,12,48]{2,1,0:T(8,128)S(1)}) fusion(bf16[128,96,12]{1,2,0:T(8,128)(2,1)} %copy.98, bf16[128,96,48]{2,1,0:T(8,128)(2,1)S(1)} %copy.99), kind=kOutput, calls=%fused_computation.110 | convolution fusion | flops 14228928 | bytes 1771776 | tf_op jit(solution)/shard_map/hki,hkj->hij/dot_general | solution.py:19
  111.0 0.2 multiply_reduce_fusion
  111.2 0.1 multiply_convert_fusion
  111.3 0.6 copy-done.2
  111.9 0.1 copy-done.6
  112.0 0.4 fusion.75
  112.4 0.3 multiply_reduce_fusion.2
  112.7 0.5 fusion.53
  113.3 0.4 copy-done.16
  113.6 1.1 fusion.14
  (49 shorter events, 0.2 us)
Async XLA Ops:
  6.5 106.2 %copy-start = (bf16[128,1024]{1,0:T(8,128)(2,1)S(1)}, bf16[128,1024]{1,0:T(8,128)(2,1)}, u32[]{:S(2)}) copy-start(bf16[128,1024]{1,0:T(8,128)(2,1)} %param.12) | copy-start | bytes 786436
  6.5 4.9 %copy-start.4 = (bf16[12,48,128]{2,1,0:T(8,128)(2,1)S(1)}, bf16[12,48,128]{2,1,0:T(8,128)(2,1)}, u32[]{:S(2)}) copy-start(bf16[12,48,128]{2,1,0:T(8,128)(2,1)} %param.7) | copy-start | bytes 442372
  6.5 31.8 %all-gather.3.cloned.1.call-start = ((), (), s32[]{:S(2)}) async-start(), calls=%async_computation.2 | async-start | bytes 1327104 | tf_op jit(solution)/shard_map/all_gather | solution.py:58
  8.3 3.5 %copy-start.10 = (f32[12,48]{1,0:T(8,128)}, f32[12,48]{1,0:T(8,128)S(1)}, u32[]{:S(2)}) copy-start(f32[12,48]{1,0:T(8,128)S(1)} %broadcast_multiply_fusion.4) | copy-start | bytes 6916
  9.5 3.1 %copy-start.14 = (f32[12,48]{1,0:T(8,128)}, f32[12,48]{1,0:T(8,128)S(1)}, u32[]{:S(2)}) copy-start(f32[12,48]{1,0:T(8,128)S(1)} %add_rsqrt_fusion.4) | copy-start | bytes 6916
  11.4 1.2 %copy-start.7 = (f32[12,48]{1,0:T(8,128)}, f32[12,48]{1,0:T(8,128)S(1)}, u32[]{:S(2)}) copy-start(f32[12,48]{1,0:T(8,128)S(1)} %broadcast_multiply_fusion.5) | copy-start | bytes 6916
  12.7 54.8 %reduce-scatter.2.cloned.1.call-start = ((), (), s32[]{:S(2)}) async-start(), calls=%async_computation.3 | async-start | bytes 1179648 | tf_op jit(solution)/shard_map/reduce_scatter | solution.py:59
  47.4 2.8 %copy-start.5 = (bf16[1,128,512]{2,1,0:T(8,128)(2,1)S(1)}, bf16[1,128,512]{2,1,0:T(8,128)(2,1)}, u32[]{:S(2)}) copy-start(bf16[1,128,512]{2,1,0:T(8,128)(2,1)} %get-tuple-element.9) | copy-start | bytes 393220
  47.4 2.9 %copy-start.11 = (f32[12,48]{1,0:T(8,128)S(1)}, f32[12,48]{1,0:T(8,128)}, u32[]{:S(2)}) copy-start(f32[12,48]{1,0:T(8,128)} %copy-done.10) | copy-start | bytes 6916
  47.4 2.9 %copy-start.15 = (f32[12,48]{1,0:T(8,128)S(1)}, f32[12,48]{1,0:T(8,128)}, u32[]{:S(2)}) copy-start(f32[12,48]{1,0:T(8,128)} %copy-done.14) | copy-start | bytes 6916
  47.4 3.0 %copy-start.17 = (bf16[2,128,128]{2,1,0:T(8,128)(2,1)S(1)}, bf16[2,128,128]{2,1,0:T(8,128)(2,1)}, u32[]{:S(2)}) copy-start(bf16[2,128,128]{2,1,0:T(8,128)(2,1)} %param.10) | copy-start | bytes 196612
  50.2 53.5 %all-gather.5.cloned.1.call-start = ((), (), s32[]{:S(2)}) async-start(), calls=%async_computation.4 | async-start | bytes 1327104 | tf_op jit(solution)/shard_map/all_gather | solution.py:65
  50.7 19.9 %copy-start.8 = (f32[12,48]{1,0:T(8,128)S(1)}, f32[12,48]{1,0:T(8,128)}, u32[]{:S(2)}) copy-start(f32[12,48]{1,0:T(8,128)} %copy-done.7) | copy-start | bytes 6916
  50.7 19.9 %copy-start.12 = (bf16[2,128,128]{2,1,0:T(8,128)(2,1)S(1)}, bf16[2,128,128]{2,1,0:T(8,128)(2,1)}, u32[]{:S(2)}) copy-start(bf16[2,128,128]{2,1,0:T(8,128)(2,1)} %param.11) | copy-start | bytes 196612
  67.5 2.9 %copy-start.3 = (f32[128,12,48]{0,1,2:T(8,128)S(1)}, f32[128,12,48]{0,1,2:T(8,128)}, u32[]{:S(2)}) copy-start(f32[128,12,48]{0,1,2:T(8,128)} %reduce-scatter.2.cloned.1.call-done) | copy-start | bytes 884740
  71.0 13.1 %copy-start.1 = (f32[12,48,128]{2,1,0:T(8,128)}, f32[12,48,128]{2,1,0:T(8,128)S(1)}, u32[]{:S(2)}) copy-start(f32[12,48,128]{2,1,0:T(8,128)S(1)} %get-tuple-element.12) | copy-start | bytes 884740
  79.5 22.8 %all-to-all-start = ((bf16[128,12,96]{0,1,2:T(8,128)(2,1)}), bf16[128,12,96]{0,1,2:T(8,128)(2,1)S(1)}, u32[]{:S(2)}, u32[]{:S(2)}) async-start(bf16[128,12,96]{0,1,2:T(8,128)(2,1)} %copy.95), calls=%async_computation.1 | async-start | bytes 786432 | tf_op jit(solution)/shard_map/all_to_all | solution.py:63
  111.0 1.0 copy-start.2
  111.0 1.0 copy-start.6
  111.0 1.0 copy-start.9
  111.0 1.0 copy-start.13
  112.7 0.9 copy-start.16
Sparse Core Ops, SparseCore 0:
  12.8 25.4 all-gather.2
  50.3 17.1 reduce-scatter.1
  72.7 30.0 all-gather.4
where the time goes:
time: 122 us; the launch traced here: 121 us
  waiting for transfers between devices  58.2 us (48%)
  local copies, waits for them, and re-layouts  20.1 us (16%)
  between operations  14.2 us (12%)
  matrix products  10.2 us (8%)
  other arithmetic  7.78 us (6%)
  blocking collectives  6.08 us (5%)
  starting transfers between devices  4.69 us (4%)
    all_gather x2, waiting for transfers between devices, body(): lax.all_gather(right_side, 'row', axis=1, tiled=True)  24.4 us
    all_to_all x1, waiting for transfers between devices, body(): lax.all_to_all(left_rows, 'row', split_axis=2, concat_axis=1, tiled=True)  17.1 us
    reduce_scatter x1, waiting for transfers between devices, body(): lax.psum_scatter(partial_rows, 'col', scatter_dimension=2, tiled=True)  16.7 us
    all_gather x2, local copies, waits for them, and re-layouts, body(): lax.all_gather(right_side, 'row', axis=1, tiled=True)  10.6 us
    all_gather x1, blocking collectives, body(): left_rows = lax.all_gather(left_side, 'col', axis=2, tiled=True)  6.08 us
    all_to_all x1, starting transfers between devices, body(): lax.all_to_all(left_rows, 'row', split_axis=2, concat_axis=1, tiled=True)  4.6 us
    dot_general x1, matrix products, contract_rows(): jnp.einsum('hik,hjk->hij', left_side, right_side, preferred_element_type=...  3.75 us
    reduce_sum x5, other arithmetic, layer_norm(): spread = jnp.mean(centred * centred, axis=along, keepdims=True)  3.23 us
  transfers between devices with their start and end apart: 4, of which 3 were waited for; matrix products, arithmetic and copies ran while one was open for 4% of the time, Pallas kernels for 0%

commit v1 on v0

--- a/solution.py
+++ b/solution.py
@@ -60,7 +60,22 @@
     stream = finish(pair, mixed_sum, gate_value, 0)
     left_side, right_side, gate_value = project(stream, 1)
     left_rows = lax.all_gather(left_side, "col", axis=2, tiled=True)
-    column_strip = lax.all_to_all(left_rows, "row", split_axis=2, concat_axis=1, tiled=True)
+    w1 = jax.lax.axis_size("row")
+    f_next = jax.lax.axis_index("row")
+    x_now, x_next = (w1, f_next)
+    row_out = left_rows.shape[2] // x_now
+    f_now = jnp.roll(left_rows, -x_next * row_out, 2)
+    parts_out = lax.slice_in_dim(f_now, 0, row_out, axis=2)
+    m = 1
+    gallery = [parts_out]
+    while m < x_now:
+        r2 = lax.slice_in_dim(f_now, m * row_out, (m + 1) * row_out, axis=2)
+        gallery.append(
+            jax.lax.ppermute(r2, "row", perm=[(h, (h + m) % x_now) for h in range(x_now)])
+        )
+        m += 1
+    z2 = jnp.concatenate(gallery[::-1], 1)
+    column_strip = jnp.roll(z2, (x_next + 1) * gallery[0].shape[1], axis=1)
     mixed_sum = contract_columns(
         column_strip, lax.all_gather(right_side, "row", axis=1, tiled=True)
     )

time: 122 us -> 127 us (1.041)
  starting transfers between devices: 4.69 us -> 7.45 us
  waiting for transfers between devices: 58.2 us -> 60.5 us
    all_to_all x1 -> x0, waiting for transfers between devices: 17.1 us -> none  [body(): lax.all_to_all(left_rows, 'row', split_axis=2, concat_axis=1, tiled=True)]
    all_gather x2, waiting for transfers between devices: 24.4 us -> 37.8 us  [body(): lax.all_gather(right_side, 'row', axis=1, tiled=True)]
    ppermute x0 -> x7, starting transfers between devices: none -> 7.36 us  [body(): jax.lax.ppermute(r2, 'row', perm=[(h, (h + m) % x_now) for h in range(x_n...]
    ppermute x0 -> x7, waiting for transfers between devices: none -> 5.92 us  [body(): jax.lax.ppermute(r2, 'row', perm=[(h, (h + m) % x_now) for h in range(x_n...]
    all_to_all x1 -> x0, starting transfers between devices: 4.6 us -> none  [body(): lax.all_to_all(left_rows, 'row', split_axis=2, concat_axis=1, tiled=True)]
    dynamic_slice x0 -> x2, local copies, waits for them, and re-layouts: none -> 1.45 us  [body(): column_strip = jnp.roll(z2, (x_next + 1) * gallery[0].shape[1], axis=1)]
    all_to_all x3 -> x0, local copies, waits for them, and re-layouts: 1.33 us -> none  [body(): lax.all_to_all(left_rows, 'row', split_axis=2, concat_axis=1, tiled=True)]
  transfers between devices with their start and end apart: 4 -> 10, of which waited for: 3 -> 4; matrix products, arithmetic and copies ran while one was open for 4% -> 3% of each run, Pallas kernels for 0% -> 0%
where the time goes in v1:
time: 127 us; the launch traced here: 126 us
  waiting for transfers between devices  60.5 us (48%)
  local copies, waits for them, and re-layouts  19.6 us (15%)
  between operations  14.3 us (11%)
  matrix products  10.2 us (8%)
  other arithmetic  7.99 us (6%)
  starting transfers between devices  7.45 us (6%)
  blocking collectives  6.07 us (5%)
    all_gather x2, waiting for transfers between devices, body(): lax.all_gather(right_side, 'row', axis=1, tiled=True)  37.8 us
    reduce_scatter x1, waiting for transfers between devices, body(): lax.psum_scatter(partial_rows, 'col', scatter_dimension=2, tiled=True)  16.7 us
    all_gather x2, local copies, waits for them, and re-layouts, body(): lax.all_gather(right_side, 'row', axis=1, tiled=True)  10.6 us
    ppermute x7, starting transfers between devices, body(): jax.lax.ppermute(r2, 'row', perm=[(h, (h + m) % x_now) for h in range(x_n...  7.36 us
    all_gather x1, blocking collectives, body(): left_rows = lax.all_gather(left_side, 'col', axis=2, tiled=True)  6.07 us
    ppermute x7, waiting for transfers between devices, body(): jax.lax.ppermute(r2, 'row', perm=[(h, (h + m) % x_now) for h in range(x_n...  5.92 us
    dot_general x1, matrix products, contract_rows(): jnp.einsum('hik,hjk->hij', left_side, right_side, preferred_element_type=...  3.74 us
    reduce_sum x5, other arithmetic, layer_norm(): spread = jnp.mean(centred * centred, axis=along, keepdims=True)  3.23 us
  transfers between devices with their start and end apart: 10, of which 4 were waited for; matrix products, arithmetic and copies ran while one was open for 3% of the time, Pallas kernels for 0%

profile of v1, /device:TPU:0, one launch (start us, length us, event | category | flops | bytes accessed | tf_op | source)
XLA Modules:
  0.0 126.1 jit_solution(12656868659926911051)
XLA Ops:
  7.2 1.1 convert_reduce_fusion
  8.3 1.2 fusion.21
  9.5 1.6 %fusion.74 = (bf16[1,128,512]{2,1,0:T(8,128)(2,1)}, bf16[1,128,512]{2,1,0:T(8,128)(2,1)S(1)}) fusion(bf16[2,128,512]{2,1,0:T(8,128)(2,1)} %param.9), kind=kLoop, calls=%fused_computation.129 | loop fusion | bytes 524288 | tf_op jit(solution)/shard_map/slice | solution.py:41
  11.2 0.1 copy.98
  11.4 0.4 convolution_bitcast_fusion.1
  11.8 0.9 fusion.39
  12.7 1.2 copy.77
  14.0 24.4 %all-gather.3.cloned.1.call-done = bf16[128,96,48]{0,2,1:T(8,128)(2,1)} async-done(((bf16[128,12,48]{0,2,1:T(8,128)(2,1)}), bf16[128,96,48]{0,2,1:T(8,128)(2,1)}) %all-gather.3.cloned.1.call-update) | async-done | bytes 1179664 | tf_op jit(solution)/shard_map/all_gather | solution.py:58
  38.4 5.3 %copy.78 = bf16[128,96,48]{2,1,0:T(8,128)(2,1)S(1)} copy(bf16[128,96,48]{0,2,1:T(8,128)(2,1)} %all-gather.3.cloned.1.call-done) | data formatting | bytes 2359296 | tf_op jit(solution)/shard_map/all_gather | solution.py:58
  43.7 3.7 %fusion.78 = f32[128,12,96]{2,1,0:T(8,128)} fusion(bf16[128,12,48]{2,1,0:T(8,128)(2,1)} %copy.77, bf16[128,96,48]{2,1,0:T(8,128)(2,1)S(1)} %copy.78), kind=kOutput, calls=%fused_computation.133 | convolution fusion | flops 14155776 | bytes 1916928 | tf_op jit(solution)/shard_map/hik,hjk->hij/dot_general | solution.py:15
  47.4 2.7 %copy.79 = f32[128,12,96]{0,1,2:T(8,128)} copy(f32[128,12,96]{2,1,0:T(8,128)} %fusion.78) | data formatting | bytes 1179648 | tf_op jit(solution)/shard_map/hik,hjk->hij/dot_general | solution.py:15
  50.3 0.1 copy.102
  50.4 0.3 fusion.11
  50.8 16.7 %reduce-scatter.2.cloned.1.call-done = f32[128,12,48]{0,1,2:T(8,128)} async-done(((f32[128,12,96]{0,1,2:T(8,128)}), f32[128,12,48]{0,1,2:T(8,128)}) %reduce-scatter.2.cloned.1.call-update) | async-done | bytes 294928 | tf_op jit(solution)/shard_map/reduce_scatter | solution.py:59
  67.5 1.2 reduce_sum.92
  68.7 0.1 copy.80
  68.8 0.1 copy.81
  68.9 1.3 %multiply_reduce_fusion.1 = f32[12,48]{0,1:T(8,128)S(1)} fusion(f32[128,12,48]{0,1,2:T(8,128)} %reduce-scatter.2.cloned.1.call-done, f32[12,48]{0,1:T(8,128)S(1)} %copy.81), kind=kLoop, calls=%fused_computation.33 | loop fusion | flops 220608 | bytes 299520 | tf_op jit(solution)/shard_map/reduce_sum | solution.py:10
  70.2 0.1 copy.82
  70.3 0.1 copy.83
  70.4 0.3 multiply_convert_fusion.1
  70.7 0.3 fusion.75
  71.0 0.3 multiply_reduce_fusion.3
  71.3 0.4 convolution_bitcast_fusion
  71.7 0.9 fusion.25
  72.5 6.1 %all_gather.10 = bf16[128,12,96]{0,2,1:T(8,128)(2,1)S(1)} all-gather(bf16[128,12,48]{0,2,1:T(8,128)(2,1)S(1)} %get-tuple-element.6), channel_id=1, replica_groups=mesh['grp'=2,'row'=8,'col'=2] {'col'}, dimensions={2}, use_global_device_ids=true | all-gather | bytes 442368 | tf_op jit(solution)/shard_map/all_gather | solution.py:62
  78.6 0.2 fusion.23
  78.8 0.1 fusion.73
  78.9 1.8 %collective-permute-start = (bf16[128,12,12]{0,2,1:T(8,128)(2,1)S(1)}, bf16[128,12,12]{0,2,1:T(8,128)(2,1)S(1)}, u32[]{:S(2)}, u32[]{:S(2)}) collective-permute-start(bf16[128,12,12]{0,2,1:T(8,128)(2,1)S(1)} %get-tuple-element.15), channel_id=1, source_target_pairs={{0,14},{2,0},{4,2},{6,4},{8,6},{10,8},{12,10},{14,12},{1,15},{3,1}... | collective-permute-start | bytes 110600 | tf_op jit(solution)/shard_map/ppermute | solution.py:74
  80.7 1.1 fusion.8
  81.8 1.6 %collective-permute-start.1 = (bf16[128,12,12]{0,2,1:T(8,128)(2,1)S(1)}, bf16[128,12,12]{0,2,1:T(8,128)(2,1)S(1)}, u32[]{:S(2)}, u32[]{:S(2)}) collective-permute-start(bf16[128,12,12]{0,2,1:T(8,128)(2,1)S(1)} %get-tuple-element.14), channel_id=1, source_target_pairs={{0,12},{2,14},{4,0},{6,2},{8,4},{10,6},{12,8},{14,10},{1,13},{3,15... | collective-permute-start | bytes 110600 | tf_op jit(solution)/shard_map/ppermute | solution.py:74
  83.4 2.7 %collective-permute-start.3 = (bf16[128,12,12]{0,2,1:T(8,128)(2,1)S(1)}, bf16[128,12,12]{0,2,1:T(8,128)(2,1)S(1)}, u32[]{:S(2)}, u32[]{:S(2)}) collective-permute-start(bf16[128,12,12]{0,2,1:T(8,128)(2,1)S(1)} %get-tuple-element.12), channel_id=1, source_target_pairs={{0,8},{2,10},{4,12},{6,14},{8,0},{10,2},{12,4},{14,6},{1,9},{3,11}... | collective-permute-start | bytes 110600 | tf_op jit(solution)/shard_map/ppermute | solution.py:74
  86.2 0.8 collective-permute-start.5
  87.0 0.4 collective-permute-start.6
  87.4 5.9 %collective-permute-done.3 = bf16[128,12,12]{0,2,1:T(8,128)(2,1)S(1)} collective-permute-done((bf16[128,12,12]{0,2,1:T(8,128)(2,1)S(1)}, bf16[128,12,12]{0,2,1:T(8,128)(2,1)S(1)}, u32[]{:S(2)}, u32[]{:S(2)}) %collective-permute-start.3) | collective-permute-done | bytes 36896 | tf_op jit(solution)/shard_map/ppermute | solution.py:74
  93.6 1.4 %copy.88 = bf16[128,96,12]{1,2,0:T(8,128)(2,1)} copy(bf16[128,96,12]{0,2,1:T(8,128)(2,1)S(1)} %constant_dynamic-slice_fusion) | data formatting | bytes 589824 | tf_op jit(solution)/shard_map/jit(_roll_dynamic)/dynamic_slice | solution.py:78
  95.1 13.4 %all-gather.5.cloned.1.call-done = bf16[128,96,48]{0,2,1:T(8,128)(2,1)} async-done(((bf16[128,12,48]{0,2,1:T(8,128)(2,1)}), bf16[128,96,48]{0,2,1:T(8,128)(2,1)}) %all-gather.5.cloned.1.call-update) | async-done | bytes 1179664 | tf_op jit(solution)/shard_map/all_gather | solution.py:80
  108.5 5.3 %copy.89 = bf16[128,96,48]{2,1,0:T(8,128)(2,1)S(1)} copy(bf16[128,96,48]{0,2,1:T(8,128)(2,1)} %all-gather.5.cloned.1.call-done) | data formatting | bytes 2359296 | tf_op jit(solution)/shard_map/all_gather | solution.py:80
  113.8 2.0 %fusion.76 = (f32[12,48]{1,0:T(8,128)S(1)}, f32[128,12,48]{2,1,0:T(8,128)S(1)}) fusion(bf16[128,96,12]{1,2,0:T(8,128)(2,1)} %copy.88, bf16[128,96,48]{2,1,0:T(8,128)(2,1)S(1)} %copy.89), kind=kOutput, calls=%fused_computation.131 | convolution fusion | flops 14228928 | bytes 1771776 | tf_op jit(solution)/shard_map/hki,hkj->hij/dot_general | solution.py:19
  115.8 0.2 multiply_reduce_fusion
  116.0 0.1 multiply_convert_fusion
  116.2 0.6 copy-done.2
  116.8 0.1 copy-done.6
  116.8 0.4 fusion.77
  117.2 0.3 multiply_reduce_fusion.2
  117.6 0.5 fusion.54
  118.1 0.4 copy-done.16
  118.5 1.1 fusion.14
  (77 shorter events, 0.6 us)
Async XLA Ops:
  6.5 111.0 %copy-start = (bf16[128,1024]{1,0:T(8,128)(2,1)S(1)}, bf16[128,1024]{1,0:T(8,128)(2,1)}, u32[]{:S(2)}) copy-start(bf16[128,1024]{1,0:T(8,128)(2,1)} %param.12) | copy-start | bytes 786436
  6.5 4.9 %copy-start.4 = (bf16[12,48,128]{2,1,0:T(8,128)(2,1)S(1)}, bf16[12,48,128]{2,1,0:T(8,128)(2,1)}, u32[]{:S(2)}) copy-start(bf16[12,48,128]{2,1,0:T(8,128)(2,1)} %param.7) | copy-start | bytes 442372
  6.5 31.8 %all-gather.3.cloned.1.call-start = ((), (), s32[]{:S(2)}) async-start(), calls=%async_computation.1 | async-start | bytes 1327104 | tf_op jit(solution)/shard_map/all_gather | solution.py:58
  8.3 3.5 %copy-start.10 = (f32[12,48]{1,0:T(8,128)}, f32[12,48]{1,0:T(8,128)S(1)}, u32[]{:S(2)}) copy-start(f32[12,48]{1,0:T(8,128)S(1)} %broadcast_multiply_fusion.4) | copy-start | bytes 6916
  9.5 3.1 %copy-start.14 = (f32[12,48]{1,0:T(8,128)}, f32[12,48]{1,0:T(8,128)S(1)}, u32[]{:S(2)}) copy-start(f32[12,48]{1,0:T(8,128)S(1)} %add_rsqrt_fusion.4) | copy-start | bytes 6916
  11.4 1.2 copy-start.7
  12.7 54.8 %reduce-scatter.2.cloned.1.call-start = ((), (), s32[]{:S(2)}) async-start(), calls=%async_computation.2 | async-start | bytes 1179648 | tf_op jit(solution)/shard_map/reduce_scatter | solution.py:59
  47.4 2.8 %copy-start.5 = (bf16[1,128,512]{2,1,0:T(8,128)(2,1)S(1)}, bf16[1,128,512]{2,1,0:T(8,128)(2,1)}, u32[]{:S(2)}) copy-start(bf16[1,128,512]{2,1,0:T(8,128)(2,1)} %get-tuple-element.16) | copy-start | bytes 393220
  47.4 3.0 %copy-start.11 = (f32[12,48]{1,0:T(8,128)S(1)}, f32[12,48]{1,0:T(8,128)}, u32[]{:S(2)}) copy-start(f32[12,48]{1,0:T(8,128)} %copy-done.10) | copy-start | bytes 6916
  47.4 3.0 %copy-start.15 = (f32[12,48]{1,0:T(8,128)S(1)}, f32[12,48]{1,0:T(8,128)}, u32[]{:S(2)}) copy-start(f32[12,48]{1,0:T(8,128)} %copy-done.14) | copy-start | bytes 6916
  47.4 3.0 %copy-start.17 = (bf16[2,128,128]{2,1,0:T(8,128)(2,1)S(1)}, bf16[2,128,128]{2,1,0:T(8,128)(2,1)}, u32[]{:S(2)}) copy-start(bf16[2,128,128]{2,1,0:T(8,128)(2,1)} %param.10) | copy-start | bytes 196612
  50.2 58.3 %all-gather.5.cloned.1.call-start = ((), (), s32[]{:S(2)}) async-start(), calls=%async_computation.3 | async-start | bytes 1327104 | tf_op jit(solution)/shard_map/all_gather | solution.py:80
  50.8 19.9 %copy-start.8 = (f32[12,48]{1,0:T(8,128)S(1)}, f32[12,48]{1,0:T(8,128)}, u32[]{:S(2)}) copy-start(f32[12,48]{1,0:T(8,128)} %copy-done.7) | copy-start | bytes 6916
  50.8 19.9 %copy-start.12 = (bf16[2,128,128]{2,1,0:T(8,128)(2,1)S(1)}, bf16[2,128,128]{2,1,0:T(8,128)(2,1)}, u32[]{:S(2)}) copy-start(bf16[2,128,128]{2,1,0:T(8,128)(2,1)} %param.11) | copy-start | bytes 196612
  67.5 2.9 %copy-start.3 = (f32[128,12,48]{0,1,2:T(8,128)S(1)}, f32[128,12,48]{0,1,2:T(8,128)}, u32[]{:S(2)}) copy-start(f32[128,12,48]{0,1,2:T(8,128)} %reduce-scatter.2.cloned.1.call-done) | copy-start | bytes 884740
  71.0 9.7 %copy-start.1 = (f32[12,48,128]{2,1,0:T(8,128)}, f32[12,48,128]{2,1,0:T(8,128)S(1)}, u32[]{:S(2)}) copy-start(f32[12,48,128]{2,1,0:T(8,128)S(1)} %get-tuple-element.19) | copy-start | bytes 884740
  78.9 7.3 %collective-permute-start = (bf16[128,12,12]{0,2,1:T(8,128)(2,1)S(1)}, bf16[128,12,12]{0,2,1:T(8,128)(2,1)S(1)}, u32[]{:S(2)}, u32[]{:S(2)}) collective-permute-start(bf16[128,12,12]{0,2,1:T(8,128)(2,1)S(1)} %get-tuple-element.15), channel_id=1, source_target_pairs={{0,14},{2,0},{4,2},{6,4},{8,6},{10,8},{12,10},{14,12},{1,15},{3,1}... | collective-permute-start | bytes 110600 | tf_op jit(solution)/shard_map/ppermute | solution.py:74
  81.8 5.2 %collective-permute-start.1 = (bf16[128,12,12]{0,2,1:T(8,128)(2,1)S(1)}, bf16[128,12,12]{0,2,1:T(8,128)(2,1)S(1)}, u32[]{:S(2)}, u32[]{:S(2)}) collective-permute-start(bf16[128,12,12]{0,2,1:T(8,128)(2,1)S(1)} %get-tuple-element.14), channel_id=1, source_target_pairs={{0,12},{2,14},{4,0},{6,2},{8,4},{10,6},{12,8},{14,10},{1,13},{3,15... | collective-permute-start | bytes 110600 | tf_op jit(solution)/shard_map/ppermute | solution.py:74
  83.4 4.0 %collective-permute-start.2 = (bf16[128,12,12]{0,2,1:T(8,128)(2,1)S(1)}, bf16[128,12,12]{0,2,1:T(8,128)(2,1)S(1)}, u32[]{:S(2)}, u32[]{:S(2)}) collective-permute-start(bf16[128,12,12]{0,2,1:T(8,128)(2,1)S(1)} %get-tuple-element.13), channel_id=1, source_target_pairs={{0,10},{2,12},{4,14},{6,0},{8,2},{10,4},{12,6},{14,8},{1,11},{3,13... | collective-permute-start | bytes 110600 | tf_op jit(solution)/shard_map/ppermute | solution.py:74
  83.4 9.9 %collective-permute-start.3 = (bf16[128,12,12]{0,2,1:T(8,128)(2,1)S(1)}, bf16[128,12,12]{0,2,1:T(8,128)(2,1)S(1)}, u32[]{:S(2)}, u32[]{:S(2)}) collective-permute-start(bf16[128,12,12]{0,2,1:T(8,128)(2,1)S(1)} %get-tuple-element.12), channel_id=1, source_target_pairs={{0,8},{2,10},{4,12},{6,14},{8,0},{10,2},{12,4},{14,6},{1,9},{3,11}... | collective-permute-start | bytes 110600 | tf_op jit(solution)/shard_map/ppermute | solution.py:74
  86.1 7.2 %collective-permute-start.4 = (bf16[128,12,12]{0,2,1:T(8,128)(2,1)S(1)}, bf16[128,12,12]{0,2,1:T(8,128)(2,1)S(1)}, u32[]{:S(2)}, u32[]{:S(2)}) collective-permute-start(bf16[128,12,12]{0,2,1:T(8,128)(2,1)S(1)} %get-tuple-element.11), channel_id=1, source_target_pairs={{0,6},{2,8},{4,10},{6,12},{8,14},{10,0},{12,2},{14,4},{1,7},{3,9},... | collective-permute-start | bytes 110600 | tf_op jit(solution)/shard_map/ppermute | solution.py:74
  86.2 7.2 %collective-permute-start.5 = (bf16[128,12,12]{0,2,1:T(8,128)(2,1)S(1)}, bf16[128,12,12]{0,2,1:T(8,128)(2,1)S(1)}, u32[]{:S(2)}, u32[]{:S(2)}) collective-permute-start(bf16[128,12,12]{0,2,1:T(8,128)(2,1)S(1)} %get-tuple-element.10), channel_id=1, source_target_pairs={{0,4},{2,6},{4,8},{6,10},{8,12},{10,14},{12,0},{14,2},{1,5},{3,7},... | collective-permute-start | bytes 110600 | tf_op jit(solution)/shard_map/ppermute | solution.py:74
  87.0 6.4 %collective-permute-start.6 = (bf16[128,12,12]{0,2,1:T(8,128)(2,1)S(1)}, bf16[128,12,12]{0,2,1:T(8,128)(2,1)S(1)}, u32[]{:S(2)}, u32[]{:S(2)}) collective-permute-start(bf16[128,12,12]{0,2,1:T(8,128)(2,1)S(1)} %get-tuple-element.9), channel_id=1, source_target_pairs={{0,2},{2,4},{4,6},{6,8},{8,10},{10,12},{12,14},{14,0},{1,3},{3,5},... | collective-permute-start | bytes 110600 | tf_op jit(solution)/shard_map/ppermute | solution.py:74
  115.8 1.0 copy-start.2
  115.8 1.0 copy-start.6
  115.8 1.0 copy-start.9
  115.8 1.0 copy-start.13
  117.5 0.9 copy-start.16
Sparse Core Ops, SparseCore 0:
  12.8 25.4 all-gather.2
  50.3 17.1 reduce-scatter.1
  86.3 22.1 all-gather.4
